TPU v7x, 32 devices: a whole 2x2x4 slice. The times are simulated.
32 devices in a mesh: band: 4 (over y, x), slab: 8 (over z, core).
Axes of the slice: x: 2, y: 2, z: 4, core: 2. Of those that a mesh axis runs over, the one named last changes fastest.
Arguments:
- band_block: float32 [4, 2, 2, 128, 128, 128], P(None, None, None, 'band', 'slab'), may hold values from -24 to 24
- material_grid: int32 [128, 128, 128], P('slab'), may hold values from 0 to 3
- inverse_permittivity: float32 [4], replicated, may hold values from 0.077 to 1
- bloch_index: int32 [1], replicated, may hold values from 0 to 7
Outputs:
- search_block: float32 [4, 2, 2, 128, 128, 128], P(None, None, None, 'band', 'slab')
- correlation: float32 [2, 8, 8], replicated
- projected: float32 [2, 8, 8], replicated
All inputs are finite; a program needn't handle non-finite values.
Results may differ from a plain program's by a relative error of at most 0.00005.
Values sent between devices are 32-bit elements; how exact they have to be, the bound alone decides.
No kernel may reach another device: no remote copies, remote signals or barrier semaphores. Data moves between devices by JAX's collectives and lax.ppermute only.
A program may use at most 192 MiB of HBM per device.

v0:
```python
from functools import partial
import math

import jax
import jax.numpy as jnp
from jax import lax
from jax.sharding import PartitionSpec as P

KPOINTS = 8


HIGHEST = lax.Precision.HIGHEST


def axis_values(length, weight, fraction, offset, extent):
    indices = offset + jnp.arange(extent, dtype=jnp.int32)
    signed = jnp.where(indices >= length // 2, indices - length, indices).astype(jnp.float32)
    return 2.0 * math.pi / length * (signed + weight * fraction)


def frame(depth_wave, height_wave, width_wave):
    depth_term = depth_wave[:, None, None]
    height_term = height_wave[None, :, None]
    width_term = width_wave[None, None, :]
    planar = jnp.sqrt(width_term * width_term + height_term * height_term)
    magnitude = jnp.sqrt(planar * planar + depth_term * depth_term)
    grid_shape = magnitude.shape
    primary = [
        jnp.broadcast_to(height_term / planar, grid_shape),
        jnp.broadcast_to(-width_term / planar, grid_shape),
        jnp.zeros(grid_shape, magnitude.dtype),
    ]
    secondary = [
        width_term * depth_term / (magnitude * planar),
        height_term * depth_term / (magnitude * planar),
        -planar / magnitude,
    ]
    return (primary, secondary, magnitude)


def curl_field(block, primary, secondary, magnitude):
    first_comp = block[:, 0]
    second_comp = block[:, 1]
    parts = [
        magnitude * (first_comp * secondary[component] - second_comp * primary[component])
        for component in range(3)
    ]
    return jnp.stack(parts, axis=1).reshape((-1,) + first_comp.shape[1:])


def project_back(spectrum, primary, secondary, magnitude, band_count):
    grouped = spectrum.reshape((band_count, 3) + spectrum.shape[1:])
    along_second = (
        grouped[:, 0] * secondary[0] + grouped[:, 1] * secondary[1] + grouped[:, 2] * secondary[2]
    )
    along_primary = (
        grouped[:, 0] * primary[0] + grouped[:, 1] * primary[1] + grouped[:, 2] * primary[2]
    )
    return jnp.stack([magnitude * along_second, -magnitude * along_primary], axis=1)


def transform(values, target, direction):
    length = values.shape[target]
    indices = jnp.arange(length, dtype=jnp.int32)
    products = indices[:, None] * indices[None, :] % length
    angles = 2.0 * math.pi / length * products.astype(jnp.float32)
    cosine = jnp.cos(angles)
    sine_table = direction * jnp.sin(angles)
    letters = "abc"
    source = letters[target - 2]
    formula = "i" + letters + "," + source + "w" + "->" + "i" + letters.replace(source, "w")
    contract = partial(jnp.einsum, formula, precision=HIGHEST)
    real_part = values[:, 0]
    imaginary = values[:, 1]
    new_real = contract(real_part, cosine) - contract(imaginary, sine_table)
    new_imag = contract(real_part, sine_table) + contract(imaginary, cosine)
    return jnp.stack([new_real, new_imag], axis=1)


def cell_values(material_grid, inverse_permittivity, grid_cells):
    inverse_cells = jnp.zeros(material_grid.shape, jnp.float32)
    for material in range(inverse_permittivity.shape[0]):
        inverse_cells = inverse_cells + jnp.where(
            material_grid == material, inverse_permittivity[material], 0.0
        )
    return inverse_cells / grid_cells


def gram_parts(left, right):
    left_real = left[:, :, 0].reshape(left.shape[0], -1)
    left_imag = left[:, :, 1].reshape(left.shape[0], -1)
    right_real = right[:, :, 0].reshape(right.shape[0], -1)
    right_imag = right[:, :, 1].reshape(right.shape[0], -1)
    inner_product = partial(jnp.einsum, "km,jm->kj", precision=HIGHEST)
    real_sum = inner_product(left_real, right_real) + inner_product(left_imag, right_imag)
    imag_sum = inner_product(left_real, right_imag) - inner_product(left_imag, right_real)
    return (real_sum, imag_sum)


def shards(band_block, material_grid, inverse_permittivity, bloch_index):
    band_groups = lax.axis_size("band")
    slab_count = lax.axis_size("slab")
    band_count = band_block.shape[0]
    depth_share = band_block.shape[3]
    row_share = band_block.shape[4]
    line_length = band_block.shape[5]
    full_depth = depth_share * band_groups
    full_rows = row_share * slab_count
    grid_cells = full_depth * full_rows * line_length
    fraction = (bloch_index[0].astype(jnp.float32) + 1.0) / KPOINTS
    row_offset = lax.axis_index("slab") * row_share
    depth_offset = lax.axis_index("band") * depth_share
    width_wave = axis_values(line_length, 0.5, fraction, 0, line_length)
    row_wave = axis_values(full_rows, 0.35, fraction, row_offset, row_share)
    point_frame = frame(
        axis_values(full_depth, 0.2, fraction, depth_offset, depth_share), row_wave, width_wave
    )
    inverse_cells = cell_values(material_grid, inverse_permittivity, grid_cells)

    def slab_operator(points):
        gathered = lax.all_to_all(points, "band", split_axis=0, concat_axis=3, tiled=True)
        primary, secondary, magnitude = frame(
            axis_values(full_depth, 0.2, fraction, 0, full_depth), row_wave, width_wave
        )
        curled = curl_field(gathered, primary, secondary, magnitude)
        spectrum = transform(transform(curled, 4, 1.0), 2, 1.0)
        spatial = (
            transform(
                lax.all_to_all(spectrum, "slab", split_axis=2, concat_axis=3, tiled=True), 3, 1.0
            )
            * inverse_cells[None, None]
        )
        returned = lax.all_to_all(
            transform(spatial, 3, -1.0), "slab", split_axis=3, concat_axis=2, tiled=True
        )
        finished = transform(transform(returned, 2, -1.0), 4, -1.0)
        local_image = project_back(finished, primary, secondary, magnitude, gathered.shape[0])
        return lax.all_to_all(local_image, "band", split_axis=3, concat_axis=0, tiled=True)

    def apply_operator(points):
        return slab_operator(points)

    image = apply_operator(band_block)
    correlation_real, correlation_imag = gram_parts(band_block, band_block)
    cross_real, cross_imag = gram_parts(band_block, image)
    correlation_real, correlation_imag, cross_real, cross_imag = lax.psum(
        (correlation_real, correlation_imag, cross_real, cross_imag), ("band", "slab")
    )
    correlation_real = correlation_real / grid_cells
    correlation_imag = correlation_imag / grid_cells
    cross_real = cross_real / grid_cells
    cross_imag = cross_imag / grid_cells
    system = jnp.concatenate(
        [
            jnp.concatenate([correlation_real, -correlation_imag], 1),
            jnp.concatenate([correlation_imag, correlation_real], 1),
        ],
        0,
    )
    right_side = jnp.concatenate([cross_real, cross_imag], 0)
    factor = jnp.linalg.cholesky(system)
    solution = jax.scipy.linalg.cho_solve((factor, True), right_side)
    mixing_real = solution[:band_count]
    mixing_imag = solution[band_count:]
    block_real = band_block[:, :, 0]
    block_imag = band_block[:, :, 1]
    combine = partial(jnp.einsum, "iabcd,ij->jabcd", precision=HIGHEST)
    residual_real = image[:, :, 0] - (
        combine(block_real, mixing_real) - combine(block_imag, mixing_imag)
    )
    residual_imag = image[:, :, 1] - (
        combine(block_real, mixing_imag) + combine(block_imag, mixing_real)
    )
    magnitude = point_frame[2]
    search_block = jnp.stack([residual_real, residual_imag], axis=2) / (magnitude * magnitude + 1.0)
    search_image = apply_operator(search_block)
    stacked = jnp.concatenate([band_block, search_block], 0)
    joint_real, joint_imag = gram_parts(stacked, search_block)
    image_real, image_imag = gram_parts(stacked, search_image)
    back_real, back_imag = gram_parts(search_block, image)
    joint_real, joint_imag, image_real, image_imag, back_real, back_imag = lax.psum(
        (joint_real, joint_imag, image_real, image_imag, back_real, back_imag), ("band", "slab")
    )
    joint_real = joint_real / grid_cells
    joint_imag = joint_imag / grid_cells
    image_real = image_real / grid_cells
    image_imag = image_imag / grid_cells
    back_real = back_real / grid_cells
    back_imag = back_imag / grid_cells
    upper_real = jnp.concatenate([correlation_real, joint_real[:band_count]], 1)
    lower_real = jnp.concatenate([joint_real[:band_count].T, joint_real[band_count:]], 1)
    upper_imag = jnp.concatenate([correlation_imag, joint_imag[:band_count]], 1)
    lower_imag = jnp.concatenate([-joint_imag[:band_count].T, joint_imag[band_count:]], 1)
    correlation = jnp.stack(
        [
            jnp.concatenate([upper_real, lower_real], 0),
            jnp.concatenate([upper_imag, lower_imag], 0),
        ],
        0,
    )
    top_real = jnp.concatenate([cross_real, image_real[:band_count]], 1)
    bottom_real = jnp.concatenate([back_real, image_real[band_count:]], 1)
    top_imag = jnp.concatenate([cross_imag, image_imag[:band_count]], 1)
    bottom_imag = jnp.concatenate([back_imag, image_imag[band_count:]], 1)
    projected = jnp.stack(
        [jnp.concatenate([top_real, bottom_real], 0), jnp.concatenate([top_imag, bottom_imag], 0)],
        0,
    )
    return (search_block, correlation, projected)


def solution(mesh):
    return jax.shard_map(
        shards,
        mesh=mesh,
        in_specs=(P(None, None, None, "band", "slab", None), P("slab", None, None), P(), P()),
        out_specs=(P(None, None, None, "band", "slab", None), P(), P()),
        check_vma=False,
    )
```

profile of v0, /device:TPU:10, one launch (start us, length us, event | category | flops | bytes accessed | tf_op | source)
XLA Modules:
  0.0 1215.9 jit_solution(13152435408415823991)
XLA Ops:
  9.0 44.1 %all-to-all-done = f32[4,2,2,32,16,128]{5,4,3,2,1,0:T(8,128)} async-done(((f32[4,2,2,32,16,128]{5,4,3,2,1,0:T(8,128)}), f32[4,2,2,32,16,128]{5,4,3,2,1,0:T(8,128)}, u32[]{:S(2)}, u32[]{:S(2)}) %all-to-all-start) | async-done | bytes 4194336 | tf_op jit(solution)/shard_map/all_to_all | solution.py:121
  102.6 129.2 %all-to-all-done.1 = f32[3,2,128,16,128]{4,3,0,1,2:T(8,128)} async-done(((f32[3,2,128,16,128]{4,3,0,1,2:T(8,128)}), f32[3,2,128,16,128]{4,3,0,1,2:T(8,128)}, u32[]{:S(2)}, u32[]{:S(2)}) %all-to-all-start.1) | async-done | bytes 6291488 | tf_op jit(solution)/shard_map/all_to_all | solution.py:129
  268.1 142.7 %all_to_all.144 = f32[3,2,16,128,128]{4,2,0,1,3:T(8,128)S(1)} all-to-all(f32[3,2,16,128,128]{4,2,0,1,3:T(8,128)S(1)} %copy.147), channel_id=1, replica_groups=mesh['band'=4,'slab'=8] {'slab'}, dimensions={3} | all-to-all | bytes 12582912 | tf_op jit(solution)/shard_map/all_to_all | solution.py:133
  457.4 11.8 convolution_bitcast_fusion.6
  469.2 11.8 fusion.95
  490.2 9.3 fusion.96
  504.6 9.7 convolution_bitcast_fusion.2
  514.3 9.3 convolution_bitcast_fusion
  523.5 9.7 fusion.98
  542.7 42.0 %all-reduce.1 = (f32[4,4]{0,1:T(4,128)S(1)}, f32[4,4]{0,1:T(4,128)S(1)}, f32[4,4]{0,1:T(4,128)S(1)}, f32[4,4]{0,1:T(4,128)S(1)}) all-reduce(f32[4,4]{0,1:T(4,128)S(1)} %fusion.95, f32[4,4]{0,1:T(4,128)S(1)} %fusion.96, f32[4,4]{0,1:T(4,128)S(1)} %fusion.100, f32[4,4]{0,1:T(4,128)S(1)} %fusion.98), channel_id=1, replica_groups=mesh['band'=4,'slab'=8] {'band','slab'}, use_global_device_ids=true, to_apply=%region_0.1 | all-reduce | flops 64 | bytes 512 | tf_op jit(solution)/shard_map/psum | solution.py:146
  610.0 49.0 %all_to_all.145 = f32[4,2,2,32,16,128]{5,4,3,1,2,0:T(8,128)S(1)} all-to-all(f32[4,2,2,32,16,128]{5,4,3,1,2,0:T(8,128)S(1)} %copy.169), channel_id=1, replica_groups=mesh['band'=4,'slab'=8] {'band'}, dimensions={0} | all-to-all | bytes 8388608 | tf_op jit(solution)/shard_map/all_to_all | solution.py:121
  691.3 139.8 %all_to_all.146 = f32[3,2,128,16,128]{4,3,0,1,2:T(8,128)S(1)} all-to-all(f32[3,2,128,16,128]{4,3,0,1,2:T(8,128)S(1)} %copy.175), channel_id=1, replica_groups=mesh['band'=4,'slab'=8] {'slab'}, dimensions={2} | all-to-all | bytes 12582912 | tf_op jit(solution)/shard_map/all_to_all | solution.py:129
  863.9 141.4 %all_to_all.147 = f32[3,2,16,128,128]{4,2,0,1,3:T(8,128)S(1)} all-to-all(f32[3,2,16,128,128]{4,2,0,1,3:T(8,128)S(1)} %copy.185), channel_id=1, replica_groups=mesh['band'=4,'slab'=8] {'slab'}, dimensions={3} | all-to-all | bytes 12582912 | tf_op jit(solution)/shard_map/all_to_all | solution.py:133
  1045.1 11.8 fusion.87
  1056.9 11.0 fusion.88
  1070.2 9.4 fusion.102
  1079.6 9.5 fusion.101
  1098.3 9.3 fusion.80
  1107.6 9.5 fusion.94
  1117.1 9.3 fusion.93
  1140.6 9.6 fusion.84
  1150.2 9.5 fusion.92
  1159.8 9.3 fusion.91
  1171.6 41.8 %all-reduce = (f32[8,4]{0,1:T(4,128)S(1)}, f32[8,4]{0,1:T(4,128)S(1)}, f32[8,4]{0,1:T(4,128)S(1)}, f32[4,4]{0,1:T(4,128)S(1)}, f32[8,4]{0,1:T(4,128)S(1)}, /*index=5*/f32[4,4]{0,1:T(4,128)S(1)}) all-reduce(f32[8,4]{0,1:T(4,128)S(1)} %fusion.93, f32[8,4]{0,1:T(4,128)S(1)} %fusion.94, ...), channel_id=1, replica_groups=mesh['band'=4,'slab'=8] {'band','slab'}, use_global_device_ids=true, to_apply=%region_7.8 | all-reduce | flops 160 | bytes 1280 | tf_op jit(solution)/shard_map/psum | solution.py:181
  (205 shorter events, 323.5 us)
Async XLA Ops:
  0.6 52.5 %all-to-all-start = ((f32[4,2,2,32,16,128]{5,4,3,2,1,0:T(8,128)}), f32[4,2,2,32,16,128]{5,4,3,2,1,0:T(8,128)}, u32[]{:S(2)}, u32[]{:S(2)}) async-start(f32[4,2,2,32,16,128]{5,4,3,2,1,0:T(8,128)} %param.4), calls=%async_computation | async-start | bytes 8388608 | tf_op jit(solution)/shard_map/all_to_all | solution.py:121
  90.9 5.8 copy-start.29
  90.9 140.9 %all-to-all-start.1 = ((f32[3,2,128,16,128]{4,3,0,1,2:T(8,128)}), f32[3,2,128,16,128]{4,3,0,1,2:T(8,128)}, u32[]{:S(2)}, u32[]{:S(2)}) async-start(f32[3,2,128,16,128]{4,3,0,1,2:T(8,128)} %copy.137), calls=%async_computation.1 | async-start | bytes 12582912 | tf_op jit(solution)/shard_map/all_to_all | solution.py:129
  445.1 54.4 %all-to-all-start.3 = ((f32[1,2,2,128,16,128]{5,4,1,2,0,3:T(8,128)}), f32[1,2,2,128,16,128]{5,4,1,2,0,3:T(8,128)}, u32[]{:S(2)}, u32[]{:S(2)}) async-start(f32[1,2,2,128,16,128]{5,4,1,2,0,3:T(8,128)} %copy.153), calls=%async_computation.3 | async-start | bytes 8388608 | tf_op jit(solution)/shard_map/all_to_all | solution.py:138
  457.4 23.6 %copy-start = (f32[4,2,2,32,16,128]{5,0,4,3,1,2:T(4,128)S(1)}, f32[4,2,2,32,16,128]{5,0,4,3,1,2:T(4,128)}, u32[]{:S(2)}) copy-start(f32[4,2,2,32,16,128]{5,0,4,3,1,2:T(4,128)} %copy.156) | copy-start | bytes 12582916
  499.5 5.1 copy-start.1
  504.6 28.6 %copy-start.7 = (f32[1,2,2,4,32,16,128]{6,3,5,4,1,2,0:T(4,128)}, f32[1,2,2,4,32,16,128]{6,3,5,4,1,2,0:T(4,128)S(1)}, u32[]{:S(2)}) copy-start(f32[1,2,2,4,32,16,128]{6,3,5,4,1,2,0:T(4,128)S(1)} %copy.305) | copy-start | bytes 12582916
  584.6 13.3 %copy-start.21 = (f32[4,4]{0,1:T(4,128)}, f32[4,4]{0,1:T(4,128)S(1)}, u32[]{:S(2)}) copy-start(f32[4,4]{0,1:T(4,128)S(1)} %get-tuple-element.54) | copy-start | bytes 196
  584.7 13.4 %copy-start.23 = (f32[4,4]{0,1:T(4,128)}, f32[4,4]{0,1:T(4,128)S(1)}, u32[]{:S(2)}) copy-start(f32[4,4]{0,1:T(4,128)S(1)} %broadcast_multiply_fusion.24) | copy-start | bytes 196
  587.7 6.5 copy-start.2
  594.2 3.8 copy-start.8
  841.9 3.6 copy-start.20
  1039.2 87.2 %all-to-all-start.7 = ((f32[1,2,2,128,16,128]{5,4,1,2,0,3:T(8,128)}), f32[1,2,2,128,16,128]{5,4,1,2,0,3:T(8,128)}, u32[]{:S(2)}, u32[]{:S(2)}) async-start(f32[1,2,2,128,16,128]{5,4,1,2,0,3:T(8,128)} %copy.191), calls=%async_computation.7 | async-start | bytes 8388608 | tf_op jit(solution)/shard_map/all_to_all | solution.py:138
  1045.1 11.8 copy-start.5
  1056.9 11.0 copy-start.3
  1070.2 37.4 %copy-start.12 = (f32[8,2,32,16,128]{4,0,3,2,1:T(8,128)}, f32[8,2,32,16,128]{4,0,3,2,1:T(8,128)S(1)}, u32[]{:S(2)}) copy-start(f32[8,2,32,16,128]{4,0,3,2,1:T(8,128)S(1)} %get-tuple-element.25) | copy-start | bytes 12582916
  1070.2 46.9 %copy-start.10 = (f32[8,2,32,16,128]{4,0,3,2,1:T(8,128)}, f32[8,2,32,16,128]{4,0,3,2,1:T(8,128)S(1)}, u32[]{:S(2)}) copy-start(f32[8,2,32,16,128]{4,0,3,2,1:T(8,128)S(1)} %get-tuple-element.24) | copy-start | bytes 12582916
  1126.4 5.1 copy-start.11
  1131.5 9.1 copy-start.13
  1159.8 9.3 copy-start.6
  1169.1 44.4 %copy-start.28 = (f32[4,4]{0,1:T(4,128)S(1)}, f32[4,4]{0,1:T(4,128)}, u32[]{:S(2)}) copy-start(f32[4,4]{0,1:T(4,128)} %copy-done.27) | copy-start | bytes 196
  1169.1 44.6 %copy-start.26 = (f32[4,4]{0,1:T(4,128)S(1)}, f32[4,4]{0,1:T(4,128)}, u32[]{:S(2)}) copy-start(f32[4,4]{0,1:T(4,128)} %copy-done.25) | copy-start | bytes 196
  1169.1 44.9 %copy-start.24 = (f32[4,4]{0,1:T(4,128)S(1)}, f32[4,4]{0,1:T(4,128)}, u32[]{:S(2)}) copy-start(f32[4,4]{0,1:T(4,128)} %copy-done.23) | copy-start | bytes 196
  1169.1 45.2 %copy-start.22 = (f32[4,4]{0,1:T(4,128)S(1)}, f32[4,4]{0,1:T(4,128)}, u32[]{:S(2)}) copy-start(f32[4,4]{0,1:T(4,128)} %copy-done.21) | copy-start | bytes 196
  (10 other events, 17.8 us)
where the time goes:
time: 1230 us; the launch traced here: 1220 us
  blocking collectives  557 us (45%)
  matrix products  369 us (30%)
  waiting for transfers between devices  173 us (14%)
  local copies, waits for them, and re-layouts  62.4 us (5%)
  other arithmetic  29 us (2%)
  starting transfers between devices  22.5 us (2%)
    all_to_all x2, blocking collectives, slab_operator(): lax.all_to_all(transform(spatial, 3, -1.0), 'slab', split_axis=3, concat_...  284 us
    all_to_all x1, blocking collectives, slab_operator(): lax.all_to_all(spectrum, 'slab', split_axis=2, concat_axis=3, tiled=True)  140 us
    all_to_all x1, waiting for transfers between devices, slab_operator(): lax.all_to_all(spectrum, 'slab', split_axis=2, concat_axis=3, tiled=True)  129 us
    dot_general x24, matrix products, transform(): new_imag = contract(real_part, sine_table) + contract(imaginary, cosine)  78.1 us
    dot_general x24, matrix products, transform(): new_real = contract(real_part, cosine) - contract(imaginary, sine_table)  76.9 us
    dot_general x5, matrix products, gram_parts(): inner_product(left_imag, right_imag)  51.4 us
    dot_general x5, matrix products, gram_parts(): inner_product(left_real, right_real) + inner_product(left_imag, right_imag)  49.9 us
    all_to_all x1, blocking collectives, slab_operator(): lax.all_to_all(points, 'band', split_axis=0, concat_axis=3, tiled=True)  49 us
  transfers between devices with their start and end apart: 4, of which 2 were waited for; matrix products, arithmetic and copies ran while one was open for 11% of the time, Pallas kernels for 0%

commit v1 on v0

v1 whole, which is shorter than its diff:
```python
from functools import partial
import math

import jax
import jax.numpy as jnp
from jax import lax
from jax.experimental import pallas as pl
from jax.experimental.pallas import tpu as pltpu
from jax.sharding import PartitionSpec as P

KPOINTS = 8


HIGH = lax.Precision.HIGH
HIGHEST = lax.Precision.HIGHEST


def axis_values(length, weight, fraction, offset, extent):
    indices = offset + jnp.arange(extent, dtype=jnp.int32)
    signed = jnp.where(indices >= length // 2, indices - length, indices).astype(jnp.float32)
    return 2.0 * math.pi / length * (signed + weight * fraction)


def frame(depth_wave, height_wave, width_wave):
    depth_term = depth_wave[:, None, None]
    height_term = height_wave[None, :, None]
    width_term = width_wave[None, None, :]
    planar = jnp.sqrt(width_term * width_term + height_term * height_term)
    magnitude = jnp.sqrt(planar * planar + depth_term * depth_term)
    grid_shape = magnitude.shape
    primary = [
        jnp.broadcast_to(height_term / planar, grid_shape),
        jnp.broadcast_to(-width_term / planar, grid_shape),
        jnp.zeros(grid_shape, magnitude.dtype),
    ]
    secondary = [
        width_term * depth_term / (magnitude * planar),
        height_term * depth_term / (magnitude * planar),
        -planar / magnitude,
    ]
    return (primary, secondary, magnitude)


def curl_field(block, primary, secondary, magnitude):
    first_comp = block[:, 0]
    second_comp = block[:, 1]
    return [
        magnitude * (first_comp * secondary[component] - second_comp * primary[component])
        for component in range(3)
    ]


def project_back(grouped, primary, secondary, magnitude):
    along_second = grouped[0] * secondary[0] + grouped[1] * secondary[1] + grouped[2] * secondary[2]
    along_primary = grouped[0] * primary[0] + grouped[1] * primary[1]
    return jnp.stack([magnitude * along_second, -magnitude * along_primary], axis=1)


def cell_values(material_grid, inverse_permittivity, grid_cells):
    inverse_cells = jnp.zeros(material_grid.shape, jnp.float32)
    for material in range(inverse_permittivity.shape[0]):
        inverse_cells = inverse_cells + jnp.where(
            material_grid == material, inverse_permittivity[material], 0.0
        )
    return inverse_cells / grid_cells


def transform(values, target, direction, precision=HIGHEST):
    length = values.shape[target]
    indices = jnp.arange(length, dtype=jnp.int32)
    products = indices[:, None] * indices[None, :] % length
    angles = 2.0 * math.pi / length * products.astype(jnp.float32)
    cosine = jnp.cos(angles)
    sine = direction * jnp.sin(angles)
    table = jnp.stack([jnp.stack([cosine, sine], 1), jnp.stack([-sine, cosine], 1)], 0)
    letters = "abc"
    source = letters[target - 2]
    formula = "ip" + letters + ",p" + source + "qw->iq" + letters.replace(source, "w")
    return jnp.einsum(formula, values, table, precision=precision)


def tile_sum(values):
    return jnp.sum(values.reshape((-1, 8) + values.shape[-1:]), axis=0)


def add_pairs(acc_ref, base, left, right):
    count = len(left)
    for i in range(count):
        for j in range(count):
            real_sum = None
            imag_sum = None
            for (lr, li), (rr, ri) in zip(left[i], right[j]):
                real_part = lr * rr + li * ri
                imag_part = lr * ri - li * rr
                real_sum = real_part if real_sum is None else real_sum + real_part
                imag_sum = imag_part if imag_sum is None else imag_sum + imag_part
            at = base + 2 * (i * count + j)
            acc_ref[at] += tile_sum(real_sum)
            acc_ref[at + 1] += tile_sum(imag_sum)


def load_bands(ref, at):
    return [
        [(ref[i, c, 0, at], ref[i, c, 1, at]) for c in range(ref.shape[1])]
        for i in range(ref.shape[0])
    ]


def clear_first(acc_ref):
    @pl.when(pl.program_id(0) == 0)
    def _():
        acc_ref[...] = jnp.zeros(acc_ref.shape, acc_ref.dtype)


def block_spec(array, size, dim):
    shape = tuple(size if d == dim else n for d, n in enumerate(array.shape))
    return pl.BlockSpec(shape, lambda s: tuple(s if d == dim else 0 for d in range(array.ndim)))


def acc_out(count, line):
    return jax.ShapeDtypeStruct((count, 8, line), jnp.float32), pl.BlockSpec(
        (count, 8, line), lambda s: (0, 0, 0)
    )


def pick(depth, size):
    return size if depth % size == 0 else 1


def first_gram(block, image):
    bands = block.shape[0]
    step = pick(block.shape[3], 4)
    pairs = 2 * bands * bands

    def kernel(b_ref, m_ref, acc_ref):
        clear_first(acc_ref)

        def one(at, carry):
            left = load_bands(b_ref, at)
            add_pairs(acc_ref, 0, left, left)
            add_pairs(acc_ref, pairs, left, load_bands(m_ref, at))
            return carry

        lax.fori_loop(0, step, one, 0)

    shape, spec = acc_out(2 * pairs, block.shape[5])
    sums = pl.pallas_call(
        kernel,
        grid=(block.shape[3] // step,),
        in_specs=[block_spec(block, step, 3), block_spec(image, step, 3)],
        out_specs=spec,
        out_shape=shape,
        name="first_gram",
    )(block, image)
    return jnp.sum(sums, axis=(1, 2))


def search_gram(block, image, scale, mixing):
    bands = block.shape[0]
    step = pick(block.shape[3], 4)
    pairs = 2 * bands * bands

    def kernel(c_ref, b_ref, m_ref, p_ref, s_ref, acc_ref):
        clear_first(acc_ref)

        def one(at, carry):
            left = load_bands(b_ref, at)
            images = load_bands(m_ref, at)
            factor = p_ref[at]
            search = []
            for j in range(bands):
                parts = []
                for c in range(2):
                    real_part, imag_part = images[j][c]
                    for i in range(bands):
                        br, bi = left[i][c]
                        cr = c_ref[i, j]
                        ci = c_ref[bands + i, j]
                        real_part = real_part - (br * cr - bi * ci)
                        imag_part = imag_part - (br * ci + bi * cr)
                    real_part = real_part * factor
                    imag_part = imag_part * factor
                    s_ref[j, c, 0, at] = real_part
                    s_ref[j, c, 1, at] = imag_part
                    parts.append((real_part, imag_part))
                search.append(parts)
            add_pairs(acc_ref, 0, left, search)
            add_pairs(acc_ref, pairs, search, search)
            add_pairs(acc_ref, 2 * pairs, search, images)
            return carry

        lax.fori_loop(0, step, one, 0)

    shape, spec = acc_out(3 * pairs, block.shape[5])
    search, sums = pl.pallas_call(
        kernel,
        grid=(block.shape[3] // step,),
        in_specs=[
            pl.BlockSpec(memory_space=pltpu.SMEM),
            block_spec(block, step, 3),
            block_spec(image, step, 3),
            block_spec(scale, step, 0),
        ],
        out_specs=[block_spec(block, step, 3), spec],
        out_shape=[jax.ShapeDtypeStruct(block.shape, jnp.float32), shape],
        name="search_gram",
    )(mixing, block, image, scale)
    return search, jnp.sum(sums, axis=(1, 2))


def field_gram(fields, weight):
    bands = fields[0].shape[0]
    depth = fields[0].shape[3]
    step = pick(depth, 4)
    pairs = 2 * bands * bands
    components = len(fields)

    def kernel(*refs):
        e_refs = refs[:components]
        w_ref = refs[components]
        acc_ref = refs[components + 1]
        clear_first(acc_ref)

        def one(at, carry):
            loaded = [load_bands(ref, at) for ref in e_refs]
            right = [sum((part[i] for part in loaded), []) for i in range(bands)]
            factor = w_ref[at]
            left = [[(a * factor, b * factor) for a, b in parts] for parts in right]
            add_pairs(acc_ref, 0, left, right)
            return carry

        lax.fori_loop(0, step, one, 0)

    shape, spec = acc_out(pairs, fields[0].shape[5])
    sums = pl.pallas_call(
        kernel,
        grid=(depth // step,),
        in_specs=[block_spec(f, step, 3) for f in fields] + [block_spec(weight, step, 0)],
        out_specs=spec,
        out_shape=shape,
        name="field_gram",
    )(*fields, weight)
    return jnp.sum(sums, axis=(1, 2))


def solve_small(system, right_side):
    rows = system.shape[0]
    wide = jnp.concatenate([system, right_side], 1)

    def kernel(m_ref, out_ref):
        values = m_ref[...]
        row_index = lax.broadcasted_iota(jnp.int32, values.shape, 0)
        for k in range(rows):
            pivot_row = values[k : k + 1, :] / values[k : k + 1, k : k + 1]
            column = values[:, k : k + 1]
            values = jnp.where(row_index == k, pivot_row, values - column * pivot_row)
        out_ref[...] = values

    solved = pl.pallas_call(
        kernel, out_shape=jax.ShapeDtypeStruct(wide.shape, jnp.float32), name="solve_small"
    )(wide)
    return solved[:, rows:]


def as_pairs(flat, bands):
    pairs = flat.reshape(bands, bands, 2)
    return pairs[:, :, 0], pairs[:, :, 1]


def shards(band_block, material_grid, inverse_permittivity, bloch_index):
    band_groups = lax.axis_size("band")
    slab_count = lax.axis_size("slab")
    band_count = band_block.shape[0]
    depth_share = band_block.shape[3]
    row_share = band_block.shape[4]
    line_length = band_block.shape[5]
    full_depth = depth_share * band_groups
    full_rows = row_share * slab_count
    grid_cells = full_depth * full_rows * line_length
    fraction = (bloch_index[0].astype(jnp.float32) + 1.0) / KPOINTS
    row_offset = lax.axis_index("slab") * row_share
    depth_offset = lax.axis_index("band") * depth_share
    width_wave = axis_values(line_length, 0.5, fraction, 0, line_length)
    row_wave = axis_values(full_rows, 0.35, fraction, row_offset, row_share)
    point_frame = frame(
        axis_values(full_depth, 0.2, fraction, depth_offset, depth_share), row_wave, width_wave
    )
    inverse_cells = cell_values(material_grid, inverse_permittivity, grid_cells)
    line_frame = frame(
        axis_values(full_depth, 0.2, fraction, 0, full_depth), row_wave, width_wave
    )

    def to_space(points, precision=HIGHEST):
        gathered = lax.all_to_all(points, "band", split_axis=0, concat_axis=3, tiled=True)
        fields = []
        for curled in curl_field(gathered, *line_frame):
            spectrum = transform(transform(curled, 2, 1.0, precision), 4, 1.0, precision)
            moved = lax.all_to_all(spectrum, "slab", split_axis=2, concat_axis=3, tiled=True)
            fields.append(transform(moved, 3, 1.0, precision))
        return fields

    def from_space(fields):
        finished = []
        for field in fields:
            returned = lax.all_to_all(
                transform(field * inverse_cells[None, None], 3, -1.0),
                "slab",
                split_axis=3,
                concat_axis=2,
                tiled=True,
            )
            finished.append(transform(transform(returned, 4, -1.0), 2, -1.0))
        local_image = project_back(finished, *line_frame)
        return lax.all_to_all(local_image, "band", split_axis=3, concat_axis=0, tiled=True)

    pair_count = 2 * band_count * band_count
    image = from_space(to_space(band_block))
    sums = lax.psum(first_gram(band_block, image), ("band", "slab")) / grid_cells
    correlation_real, correlation_imag = as_pairs(sums[:pair_count], band_count)
    cross_real, cross_imag = as_pairs(sums[pair_count:], band_count)
    system = jnp.concatenate(
        [
            jnp.concatenate([correlation_real, -correlation_imag], 1),
            jnp.concatenate([correlation_imag, correlation_real], 1),
        ],
        0,
    )
    right_side = jnp.concatenate([cross_real, cross_imag], 0)
    mixing = solve_small(system, right_side)
    magnitude = point_frame[2]
    scale = 1.0 / (magnitude * magnitude + 1.0)
    search_block, search_sums = search_gram(band_block, image, scale, mixing)
    rows_here = full_rows // band_groups
    fields = [
        lax.all_to_all(field[:, None], "band", split_axis=4, concat_axis=0, tiled=True)
        for field in to_space(search_block, HIGH)
    ]
    weight = lax.dynamic_slice_in_dim(
        inverse_cells, lax.axis_index("band") * rows_here, rows_here, 1
    )
    field_sums = field_gram(fields, weight)
    sums = (
        lax.psum(jnp.concatenate([search_sums, field_sums]), ("band", "slab")) / grid_cells
    )
    joint_real, joint_imag = as_pairs(sums[:pair_count], band_count)
    own_real, own_imag = as_pairs(sums[pair_count : 2 * pair_count], band_count)
    back_real, back_imag = as_pairs(sums[2 * pair_count : 3 * pair_count], band_count)
    last_real, last_imag = as_pairs(sums[3 * pair_count :], band_count)
    correlation = jnp.stack(
        [
            jnp.block([[correlation_real, joint_real], [joint_real.T, own_real]]),
            jnp.block([[correlation_imag, joint_imag], [-joint_imag.T, own_imag]]),
        ],
        0,
    )
    projected = jnp.stack(
        [
            jnp.block([[cross_real, back_real.T], [back_real, last_real]]),
            jnp.block([[cross_imag, -back_imag.T], [back_imag, last_imag]]),
        ],
        0,
    )
    return (search_block, correlation, projected)


def solution(mesh):
    return jax.shard_map(
        shards,
        mesh=mesh,
        in_specs=(P(None, None, None, "band", "slab", None), P("slab", None, None), P(), P()),
        out_specs=(P(None, None, None, "band", "slab", None), P(), P()),
        check_vma=False,
    )
```

time: 1230 us -> 899 us (0.73)
  blocking collectives: 557 us -> 133 us
  matrix products: 369 us -> 59.7 us
  waiting for transfers between devices: 173 us -> 469 us
  starting transfers between devices: 22.5 us -> 87.6 us
  Pallas kernels: 0 us -> 28.7 us
  local copies, waits for them, and re-layouts: 62.4 us -> 86 us
    all_to_all x4 -> x1, blocking collectives: 473 us -> 50.4 us  [to_space(): lax.all_to_all(points, 'band', split_axis=0, concat_axis=3, tiled=True)]
    dot_general x72 -> x27, matrix products: 369 us -> 59.7 us  [transform(): return jnp.einsum(formula, values, table, precision=precision)]
    all_to_all x4 -> x14, waiting for transfers between devices: 173 us -> 469 us  [the longest x6 220 us: to_space(): lax.all_to_all(spectrum, 'slab', split_axis=2, concat_axis=3, tiled=True)]
    all_to_all x4 -> x14, starting transfers between devices: 22.5 us -> 87.6 us  [the longest x6 38.6 us: to_space(): lax.all_to_all(spectrum, 'slab', split_axis=2, concat_axis=3, tiled=True)]
    pallas_call x0 -> x4, Pallas kernels: none -> 28.7 us  [the longest x1 12.1 us: search_gram(): pl.pallas_call(kernel, grid=(block.shape[3] // step,), in_specs=[pl.Block...]
    transpose x1 -> x9, local copies, waits for them, and re-layouts: 0.09 us -> 24.1 us  [transform(): return jnp.einsum(formula, values, table, precision=precision)]
    another operation x4 -> x0, local copies, waits for them, and re-layouts: 17.2 us -> none  [transform(): return jnp.stack([new_real, new_imag], axis=1)]
    all_to_all x8 -> x21, local copies, waits for them, and re-layouts: 21.5 us -> 35.5 us  [the longest x3 10.9 us: shards(): lax.all_to_all(field[:, None], 'band', split_axis=4, concat_axis=0, tiled...]
  transfers between devices with their start and end apart: 4 -> 14, of which waited for: 2 -> 14; matrix products, arithmetic and copies ran while one was open for 11% -> 12% of each run, Pallas kernels for 0% -> 0%
where the time goes in v1:
time: 899 us; the launch traced here: 890 us
  waiting for transfers between devices  469 us (52%)
  blocking collectives  133 us (15%)
  starting transfers between devices  87.6 us (10%)
  local copies, waits for them, and re-layouts  86 us (10%)
  matrix products  59.7 us (7%)
  Pallas kernels  28.7 us (3%)
  other arithmetic  23.7 us (3%)
    all_to_all x6, waiting for transfers between devices, to_space(): lax.all_to_all(spectrum, 'slab', split_axis=2, concat_axis=3, tiled=True)  220 us
    all_to_all x3, waiting for transfers between devices, from_space(): lax.all_to_all(transform(field * inverse_cells[None, None], 3, -1.0), 'sl...  109 us
    dot_general x27, matrix products, transform(): return jnp.einsum(formula, values, table, precision=precision)  59.7 us
    all_to_all x3, waiting for transfers between devices, shards(): lax.all_to_all(field[:, None], 'band', split_axis=4, concat_axis=0, tiled...  51.8 us
    all_to_all x1, blocking collectives, to_space(): lax.all_to_all(points, 'band', split_axis=0, concat_axis=3, tiled=True)  50.4 us
    all_to_all x1, waiting for transfers between devices, from_space(): lax.all_to_all(local_image, 'band', split_axis=3, concat_axis=0, tiled=True)  46.5 us
    all_to_all x1, waiting for transfers between devices, to_space(): lax.all_to_all(points, 'band', split_axis=0, concat_axis=3, tiled=True)  42 us
    psum x1, blocking collectives, shards(): lax.psum(first_gram(band_block, image), ('band', 'slab')) / grid_cells  41.6 us
  transfers between devices with their start and end apart: 14, of which 14 were waited for; matrix products, arithmetic and copies ran while one was open for 12% of the time, Pallas kernels for 0%

profile of v1, /device:TPU:10, one launch (start us, length us, event | category | flops | bytes accessed | tf_op | source)
XLA Modules:
  0.0 889.8 jit_solution(5370330054866795547)
XLA Ops:
  11.1 42.0 %all-to-all-done = f32[4,2,2,32,16,128]{5,4,3,2,1,0:T(8,128)} async-done(((f32[4,2,2,32,16,128]{5,4,3,2,1,0:T(8,128)}), f32[4,2,2,32,16,128]{5,4,3,2,1,0:T(8,128)}, u32[]{:S(2)}, u32[]{:S(2)}) %all-to-all-start) | async-done | bytes 4194336 | tf_op jit(solution)/shard_map/all_to_all | solution.py:294
  81.5 35.7 %all-to-all-done.5 = f32[1,2,128,16,128]{4,3,1,0,2:T(8,128)S(1)} async-done(((f32[1,2,128,16,128]{4,3,1,0,2:T(8,128)}), f32[1,2,128,16,128]{4,3,1,0,2:T(8,128)S(1)}, u32[]{:S(2)}, u32[]{:S(2)}) %all-to-all-start.5) | async-done | bytes 2097184 | tf_op jit(solution)/shard_map/all_to_all | solution.py:298
  135.2 35.8 %all-to-all-done.3 = f32[1,2,128,16,128]{4,3,1,0,2:T(8,128)S(1)} async-done(((f32[1,2,128,16,128]{4,3,1,0,2:T(8,128)}), f32[1,2,128,16,128]{4,3,1,0,2:T(8,128)S(1)}, u32[]{:S(2)}, u32[]{:S(2)}) %all-to-all-start.3) | async-done | bytes 2097184 | tf_op jit(solution)/shard_map/all_to_all | solution.py:298
  172.3 7.9 all-to-all-start.1
  192.1 33.7 %all-to-all-done.1 = f32[1,2,128,16,128]{4,3,1,0,2:T(8,128)} async-done(((f32[1,2,128,16,128]{4,3,1,0,2:T(8,128)}), f32[1,2,128,16,128]{4,3,1,0,2:T(8,128)}, u32[]{:S(2)}, u32[]{:S(2)}) %all-to-all-start.1) | async-done | bytes 2097184 | tf_op jit(solution)/shard_map/all_to_all | solution.py:298
  225.8 7.8 all-to-all-start.6
  242.1 37.1 %all-to-all-done.6 = f32[1,2,16,128,128]{4,2,1,0,3:T(8,128)} async-done(((f32[1,2,16,128,128]{4,2,1,0,3:T(8,128)}), f32[1,2,16,128,128]{4,2,1,0,3:T(8,128)}, u32[]{:S(2)}, u32[]{:S(2)}) %all-to-all-start.6) | async-done | bytes 2097184 | tf_op jit(solution)/shard_map/all_to_all | solution.py:305
  279.2 7.8 all-to-all-start.4
  295.5 37.1 %all-to-all-done.4 = f32[1,2,16,128,128]{4,2,1,0,3:T(8,128)} async-done(((f32[1,2,16,128,128]{4,2,1,0,3:T(8,128)}), f32[1,2,16,128,128]{4,2,1,0,3:T(8,128)}, u32[]{:S(2)}, u32[]{:S(2)}) %all-to-all-start.4) | async-done | bytes 2097184 | tf_op jit(solution)/shard_map/all_to_all | solution.py:305
  332.6 8.0 all-to-all-start.2
  351.5 34.5 %all-to-all-done.2 = f32[1,2,16,128,128]{4,2,1,0,3:T(8,128)} async-done(((f32[1,2,16,128,128]{4,2,1,0,3:T(8,128)}), f32[1,2,16,128,128]{4,2,1,0,3:T(8,128)}, u32[]{:S(2)}, u32[]{:S(2)}) %all-to-all-start.2) | async-done | bytes 2097184 | tf_op jit(solution)/shard_map/all_to_all | solution.py:305
  407.4 46.5 %all-to-all-done.7 = f32[1,2,2,128,16,128]{5,4,2,1,0,3:T(8,128)} async-done(((f32[1,2,2,128,16,128]{5,4,2,1,0,3:T(8,128)}), f32[1,2,2,128,16,128]{5,4,2,1,0,3:T(8,128)}, u32[]{:S(2)}, u32[]{:S(2)}) %all-to-all-start.7) | async-done | bytes 4194336 | tf_op jit(solution)/shard_map/all_to_all | solution.py:314
  458.6 8.3 first_gram.1
  468.4 41.6 %psum.14 = f32[64]{0:T(128)S(1)} all-reduce(f32[64]{0:T(128)S(1)} %reduce_sum.27), channel_id=1, replica_groups=mesh['band'=4,'slab'=8] {'band','slab'}, use_global_device_ids=true, to_apply=%region_1.2 | all-reduce | flops 64 | bytes 512 | tf_op jit(solution)/shard_map/psum | solution.py:318
  514.5 12.1 %search_gram.1 = (f32[4,2,2,32,16,128]{5,4,3,2,1,0:T(8,128)}, f32[96,8,128]{2,1,0:T(8,128)}) custom-call(f32[8,4]{1,0:T(8,128)} %slice.155.c_ref, f32[4,2,2,32,16,128]{5,4,3,2,1,0:T(8,128)} %b_ref.3, f32[4,2,2,32,16,128]{5,4,3,2,1,0:T(8,128)} %bitcast.468, f32[32,16,128]{2,1,0:T(8,128)} %add_divide_fusion.p_ref), custom_call_target="tpu_custom_call" | custom-call | tf_op jit(solution)/shard_map/search_gram/pallas_call | solution.py:195
  526.6 50.4 %all_to_all.243 = f32[4,2,2,32,16,128]{5,4,3,2,1,0:T(8,128)S(1)} all-to-all(f32[4,2,2,32,16,128]{5,4,3,2,1,0:T(8,128)} %get-tuple-element.2), channel_id=1, replica_groups=mesh['band'=4,'slab'=8] {'band'}, dimensions={0} | all-to-all | bytes 8388608 | tf_op jit(solution)/shard_map/all_to_all | solution.py:294
  599.5 37.4 %all-to-all-done.13 = f32[1,2,128,16,128]{4,3,1,0,2:T(8,128)S(1)} async-done(((f32[1,2,128,16,128]{4,3,1,0,2:T(8,128)}), f32[1,2,128,16,128]{4,3,1,0,2:T(8,128)S(1)}, u32[]{:S(2)}, u32[]{:S(2)}) %all-to-all-start.13) | async-done | bytes 2097184 | tf_op jit(solution)/shard_map/all_to_all | solution.py:298
  653.5 37.3 %all-to-all-done.11 = f32[1,2,128,16,128]{4,3,1,0,2:T(8,128)S(1)} async-done(((f32[1,2,128,16,128]{4,3,1,0,2:T(8,128)}), f32[1,2,128,16,128]{4,3,1,0,2:T(8,128)S(1)}, u32[]{:S(2)}, u32[]{:S(2)}) %all-to-all-start.11) | async-done | bytes 2097184 | tf_op jit(solution)/shard_map/all_to_all | solution.py:298
  692.1 7.2 all-to-all-start.9
  705.1 39.8 %all-to-all-done.9 = f32[1,2,128,16,128]{4,3,1,0,2:T(8,128)S(1)} async-done(((f32[1,2,128,16,128]{4,3,1,0,2:T(8,128)}), f32[1,2,128,16,128]{4,3,1,0,2:T(8,128)S(1)}, u32[]{:S(2)}, u32[]{:S(2)}) %all-to-all-start.9) | async-done | bytes 2097184 | tf_op jit(solution)/shard_map/all_to_all | solution.py:298
  756.2 19.0 %all-to-all-done.14 = f32[1,1,2,16,128,128]{5,3,2,1,0,4:T(8,128)S(1)} async-done(((f32[1,1,2,16,128,128]{5,3,2,1,0,4:T(8,128)}), f32[1,1,2,16,128,128]{5,3,2,1,0,4:T(8,128)S(1)}, u32[]{:S(2)}, u32[]{:S(2)}) %all-to-all-start.14) | async-done | bytes 2097184 | tf_op jit(solution)/shard_map/all_to_all | solution.py:335
  785.9 18.2 %all-to-all-done.12 = f32[1,1,2,16,128,128]{5,3,2,1,0,4:T(8,128)} async-done(((f32[1,1,2,16,128,128]{5,3,2,1,0,4:T(8,128)}), f32[1,1,2,16,128,128]{5,3,2,1,0,4:T(8,128)}, u32[]{:S(2)}, u32[]{:S(2)}) %all-to-all-start.12) | async-done | bytes 2097184 | tf_op jit(solution)/shard_map/all_to_all | solution.py:335
  818.8 14.6 %all-to-all-done.10 = f32[1,1,2,16,128,128]{5,3,2,1,0,4:T(8,128)} async-done(((f32[1,1,2,16,128,128]{5,3,2,1,0,4:T(8,128)}), f32[1,1,2,16,128,128]{5,3,2,1,0,4:T(8,128)}, u32[]{:S(2)}, u32[]{:S(2)}) %all-to-all-start.10) | async-done | bytes 2097184 | tf_op jit(solution)/shard_map/all_to_all | solution.py:335
  845.2 41.3 %psum.15 = f32[128]{0:T(128)S(1)} all-reduce(f32[128]{0:T(128)S(1)} %pad_maximum_fusion.8), channel_id=1, replica_groups=mesh['band'=4,'slab'=8] {'band','slab'}, use_global_device_ids=true, to_apply=%region_4.5 | all-reduce | flops 128 | bytes 1024 | tf_op jit(solution)/shard_map/psum | solution.py:343
  (181 shorter events, 226.5 us)
Async XLA Ops:
  0.6 52.5 %all-to-all-start = ((f32[4,2,2,32,16,128]{5,4,3,2,1,0:T(8,128)}), f32[4,2,2,32,16,128]{5,4,3,2,1,0:T(8,128)}, u32[]{:S(2)}, u32[]{:S(2)}) async-start(f32[4,2,2,32,16,128]{5,4,3,2,1,0:T(8,128)} %b_ref.3), calls=%async_computation | async-start | bytes 8388608 | tf_op jit(solution)/shard_map/all_to_all | solution.py:294
  11.1 45.6 %copy-start = (f32[128,16,128]{2,0,1:T(8,128)}, f32[128,16,128]{2,0,1:T(8,128)S(1)}, u32[]{:S(2)}) copy-start(f32[128,16,128]{2,0,1:T(8,128)S(1)} %get-tuple-element.35) | copy-start | bytes 3145732
  11.1 45.6 %copy-start.3 = (f32[128,16,128]{2,0,1:T(8,128)}, f32[128,16,128]{2,0,1:T(8,128)S(1)}, u32[]{:S(2)}) copy-start(f32[128,16,128]{2,0,1:T(8,128)S(1)} %get-tuple-element.37) | copy-start | bytes 3145732
  11.1 45.6 %copy-start.6 = (f32[128,16,128]{2,0,1:T(8,128)}, f32[128,16,128]{2,0,1:T(8,128)S(1)}, u32[]{:S(2)}) copy-start(f32[128,16,128]{2,0,1:T(8,128)S(1)} %get-tuple-element.38) | copy-start | bytes 3145732
  53.1 3.6 copy-start.9
  65.7 51.4 %all-to-all-start.5 = ((f32[1,2,128,16,128]{4,3,1,0,2:T(8,128)}), f32[1,2,128,16,128]{4,3,1,0,2:T(8,128)S(1)}, u32[]{:S(2)}, u32[]{:S(2)}) async-start(f32[1,2,128,16,128]{4,3,1,0,2:T(8,128)} %copy.106), calls=%async_computation.5 | async-start | bytes 4194304 | tf_op jit(solution)/shard_map/all_to_all | solution.py:298
  118.5 52.5 %all-to-all-start.3 = ((f32[1,2,128,16,128]{4,3,1,0,2:T(8,128)}), f32[1,2,128,16,128]{4,3,1,0,2:T(8,128)S(1)}, u32[]{:S(2)}, u32[]{:S(2)}) async-start(f32[1,2,128,16,128]{4,3,1,0,2:T(8,128)} %copy.95), calls=%async_computation.3 | async-start | bytes 4194304 | tf_op jit(solution)/shard_map/all_to_all | solution.py:298
  135.2 45.1 %copy-start.25 = (f32[4]{0:T(128)S(1)}, f32[4]{0:T(128)}, u32[]{:S(2)}) copy-start(f32[4]{0:T(128)} %param.6) | copy-start | bytes 52
  172.3 53.5 %all-to-all-start.1 = ((f32[1,2,128,16,128]{4,3,1,0,2:T(8,128)}), f32[1,2,128,16,128]{4,3,1,0,2:T(8,128)}, u32[]{:S(2)}, u32[]{:S(2)}) async-start(f32[1,2,128,16,128]{4,3,1,0,2:T(8,128)} %copy.84), calls=%async_computation.1 | async-start | bytes 4194304 | tf_op jit(solution)/shard_map/all_to_all | solution.py:298
  180.3 4.9 copy-start.18
  225.8 53.4 %all-to-all-start.6 = ((f32[1,2,16,128,128]{4,2,1,0,3:T(8,128)}), f32[1,2,16,128,128]{4,2,1,0,3:T(8,128)}, u32[]{:S(2)}, u32[]{:S(2)}) async-start(f32[1,2,16,128,128]{4,2,1,0,3:T(8,128)} %copy.111), calls=%async_computation.6 | async-start | bytes 4194304 | tf_op jit(solution)/shard_map/all_to_all | solution.py:305
  279.2 53.4 %all-to-all-start.4 = ((f32[1,2,16,128,128]{4,2,1,0,3:T(8,128)}), f32[1,2,16,128,128]{4,2,1,0,3:T(8,128)}, u32[]{:S(2)}, u32[]{:S(2)}) async-start(f32[1,2,16,128,128]{4,2,1,0,3:T(8,128)} %copy.100), calls=%async_computation.4 | async-start | bytes 4194304 | tf_op jit(solution)/shard_map/all_to_all | solution.py:305
  332.6 53.4 %all-to-all-start.2 = ((f32[1,2,16,128,128]{4,2,1,0,3:T(8,128)}), f32[1,2,16,128,128]{4,2,1,0,3:T(8,128)}, u32[]{:S(2)}, u32[]{:S(2)}) async-start(f32[1,2,16,128,128]{4,2,1,0,3:T(8,128)} %copy.89), calls=%async_computation.2 | async-start | bytes 4194304 | tf_op jit(solution)/shard_map/all_to_all | solution.py:305
  387.9 4.0 copy-start.15
  392.0 3.4 copy-start.22
  401.0 5.6 copy-start.24
  401.0 52.9 %all-to-all-start.7 = ((f32[1,2,2,128,16,128]{5,4,2,1,0,3:T(8,128)}), f32[1,2,2,128,16,128]{5,4,2,1,0,3:T(8,128)}, u32[]{:S(2)}, u32[]{:S(2)}) async-start(f32[1,2,2,128,16,128]{5,4,2,1,0,3:T(8,128)} %copy.116), calls=%async_computation.7 | async-start | bytes 8388608 | tf_op jit(solution)/shard_map/all_to_all | solution.py:314
  577.4 2.2 copy-start.11
  587.7 49.2 %all-to-all-start.13 = ((f32[1,2,128,16,128]{4,3,1,0,2:T(8,128)}), f32[1,2,128,16,128]{4,3,1,0,2:T(8,128)S(1)}, u32[]{:S(2)}, u32[]{:S(2)}) async-start(f32[1,2,128,16,128]{4,3,1,0,2:T(8,128)} %copy.137), calls=%async_computation.13 | async-start | bytes 4194304 | tf_op jit(solution)/shard_map/all_to_all | solution.py:298
  638.2 52.5 %all-to-all-start.11 = ((f32[1,2,128,16,128]{4,3,1,0,2:T(8,128)}), f32[1,2,128,16,128]{4,3,1,0,2:T(8,128)S(1)}, u32[]{:S(2)}, u32[]{:S(2)}) async-start(f32[1,2,128,16,128]{4,3,1,0,2:T(8,128)} %copy.130), calls=%async_computation.11 | async-start | bytes 4194304 | tf_op jit(solution)/shard_map/all_to_all | solution.py:298
  692.1 52.8 %all-to-all-start.9 = ((f32[1,2,128,16,128]{4,3,1,0,2:T(8,128)}), f32[1,2,128,16,128]{4,3,1,0,2:T(8,128)S(1)}, u32[]{:S(2)}, u32[]{:S(2)}) async-start(f32[1,2,128,16,128]{4,3,1,0,2:T(8,128)} %copy.123), calls=%async_computation.9 | async-start | bytes 4194304 | tf_op jit(solution)/shard_map/all_to_all | solution.py:298
  746.2 28.9 %all-to-all-start.14 = ((f32[1,1,2,16,128,128]{5,3,2,1,0,4:T(8,128)}), f32[1,1,2,16,128,128]{5,3,2,1,0,4:T(8,128)S(1)}, u32[]{:S(2)}, u32[]{:S(2)}) async-start(f32[1,1,2,16,128,128]{5,3,2,1,0,4:T(8,128)} %copy.140), calls=%async_computation.14 | async-start | bytes 4194304 | tf_op jit(solution)/shard_map/all_to_all | solution.py:335
  775.2 29.0 %all-to-all-start.12 = ((f32[1,1,2,16,128,128]{5,3,2,1,0,4:T(8,128)}), f32[1,1,2,16,128,128]{5,3,2,1,0,4:T(8,128)}, u32[]{:S(2)}, u32[]{:S(2)}) async-start(f32[1,1,2,16,128,128]{5,3,2,1,0,4:T(8,128)} %copy.133), calls=%async_computation.12 | async-start | bytes 4194304 | tf_op jit(solution)/shard_map/all_to_all | solution.py:335
  804.2 29.2 %all-to-all-start.10 = ((f32[1,1,2,16,128,128]{5,3,2,1,0,4:T(8,128)}), f32[1,1,2,16,128,128]{5,3,2,1,0,4:T(8,128)}, u32[]{:S(2)}, u32[]{:S(2)}) async-start(f32[1,1,2,16,128,128]{5,3,2,1,0,4:T(8,128)} %copy.126), calls=%async_computation.10 | async-start | bytes 4194304 | tf_op jit(solution)/shard_map/all_to_all | solution.py:335
  (16 other events, 25.9 us)
